TPU v7x, 256 devices: a whole 4x4x8 slice. The times are simulated.
256 devices in a mesh: ctx: 64 (over z, y, core), hg: 4 (over x).
Axes of the slice: x: 4, y: 4, z: 8, core: 2. Of those that a mesh axis runs over, the one named last changes fastest.
Arguments:
- doc_ids: int32 [32768], P('ctx'), may hold values from 0 to 63, never falling along the last dimension, each value on 1 to 1024 neighbouring positions
- rotated_queries: bfloat16 [32768, 2048], P('ctx', 'hg'), may hold values from -6 to 6
- rotated_keys: bfloat16 [32768, 512], P('ctx', 'hg'), may hold values from -6 to 6
- value_matrix: bfloat16 [32768, 512], P('ctx', 'hg'), may hold values from -6 to 6
- out_proj: bfloat16 [4096, 2048], P('ctx', 'hg'), may hold values from -0.125 to 0.125
- cotangent: bfloat16 [32768, 4096], P('ctx'), may hold values from -16 to 16
Outputs:
- layer_output: bfloat16 [32768, 4096], P('ctx', 'hg')
- query_grad: bfloat16 [32768, 2048], P('ctx', 'hg')
- key_gradient: bfloat16 [32768, 512], P('ctx', 'hg')
- value_gradient: bfloat16 [32768, 512], P('ctx', 'hg')
- proj_grad: bfloat16 [4096, 2048], P('ctx', 'hg')
Inputs may be any that keep to these rules, and one draw needn't show every extreme that they name: `doc_ids`: document ids in token order, never falling; every document has 1 to 1024 tokens and one has exactly 1024.
All inputs are finite; a program needn't handle non-finite values.
Results may differ from a plain program's by a relative error of at most 0.013.
Values may be sent and summed in bfloat16 or wider, within the bound.
A program may use at most 128 MiB of HBM per device.

v0:
```python
import jax
import jax.numpy as jnp
from jax import lax
from jax.sharding import PartitionSpec as P

HEAD_SIZE = 128
TOK_DEV = 512
DOC_MOST = 1024


def from_behind(value, axis, by):
    devices = lax.axis_size(axis)
    pairs = [(i, i + by) for i in range(devices) if 0 <= i + by < devices]
    return lax.ppermute(value, axis, pairs)


def contract_last(left_side, right_side):
    return lax.dot_general(
        left_side, right_side, (((1,), (1,)), ((), ())), preferred_element_type=jnp.float32
    )


def contract_first(left_side, right_side):
    return lax.dot_general(
        left_side, right_side, (((0,), (0,)), ((), ())), preferred_element_type=jnp.float32
    )


def body(doc_ids, rotated_queries, rotated_keys, value_matrix, out_proj, cotangent):
    row_count = rotated_queries.shape[0]
    head_count = rotated_queries.shape[1] // HEAD_SIZE
    kv_count = rotated_keys.shape[1] // HEAD_SIZE
    group_length = head_count // kv_count
    steps_back = DOC_MOST // TOK_DEV
    score_scale = HEAD_SIZE ** (-0.5)
    device_index = lax.axis_index("ctx")
    earlier = [(rotated_keys, value_matrix, doc_ids)]
    for offset in range(1, steps_back + 1):
        earlier.append(from_behind((rotated_keys, value_matrix, doc_ids), "ctx", offset))
    ordered = earlier[::-1]
    key_cat = jnp.concatenate([member[0] for member in ordered], 0)
    value_cat = jnp.concatenate([member[1] for member in ordered], 0)
    doc_cat = jnp.concatenate([member[2] for member in ordered], 0)
    key_width = key_cat.shape[0]
    query_pos = jnp.arange(row_count, dtype=jnp.int32)
    column_pos = jnp.arange(key_width, dtype=jnp.int32)
    key_pos = column_pos - steps_back * row_count
    first_valid = (steps_back - device_index) * row_count
    allowed = (
        (doc_ids[:, None] == doc_cat[None, :])
        & (key_pos[None, :] <= query_pos[:, None])
        & (column_pos[None, :] >= first_valid)
    )
    outputs = []
    probs_list = []
    for head_index in range(head_count):
        kv_index = head_index // group_length
        query_head = rotated_queries[:, head_index * HEAD_SIZE : (head_index + 1) * HEAD_SIZE]
        key_head = key_cat
        value_head = value_cat
        scores = contract_last(query_head, key_head) * score_scale
        masked = jnp.where(allowed, scores, -jnp.inf)
        row_max = jnp.max(masked, axis=1, keepdims=True)
        row_sum = jnp.sum(jnp.where(allowed, jnp.exp(masked - row_max), 0.0), axis=1, keepdims=True)
        log_total = row_max + jnp.log(row_sum)
        weights = jnp.where(allowed, jnp.exp(masked - log_total), 0.0).astype(jnp.bfloat16)
        probs_list.append(weights)
        outputs.append(
            jnp.dot(weights, value_head, preferred_element_type=jnp.float32).astype(jnp.bfloat16)
        )
    attended = jnp.concatenate(outputs, 1)
    partial_value = contract_last(attended, lax.all_gather(out_proj, "ctx", axis=0, tiled=True))
    layer_output = lax.psum_scatter(
        partial_value.astype(jnp.bfloat16), "hg", scatter_dimension=1, tiled=True
    )
    columns = cotangent
    attention_gradient = jnp.dot(
        columns,
        lax.all_gather(out_proj, "ctx", axis=0, tiled=True),
        preferred_element_type=jnp.float32,
    ).astype(jnp.bfloat16)
    columns = cotangent
    proj_grad = lax.psum_scatter(
        contract_first(columns, attended), "ctx", scatter_dimension=0, tiled=True
    ).astype(jnp.bfloat16)
    key_parts = [jnp.zeros((key_width, HEAD_SIZE), jnp.float32)]
    value_parts = [jnp.zeros((key_width, HEAD_SIZE), jnp.float32)]
    query_grads = []
    for head_index in range(head_count):
        kv_index = head_index // group_length
        query_head = rotated_queries[:, head_index * HEAD_SIZE : (head_index + 1) * HEAD_SIZE]
        key_head = key_cat
        value_head = value_cat
        grad_head = attention_gradient[:, head_index * HEAD_SIZE : (head_index + 1) * HEAD_SIZE]
        weights = probs_list[head_index]
        row_delta = jnp.sum(
            grad_head.astype(jnp.float32) * outputs[head_index].astype(jnp.float32),
            axis=1,
            keepdims=True,
        )
        grad_dots = contract_last(grad_head, value_head)
        shifted = (weights.astype(jnp.float32) * (grad_dots - row_delta) * score_scale).astype(
            jnp.bfloat16
        )
        query_grads.append(
            jnp.dot(shifted, key_head, preferred_element_type=jnp.float32).astype(jnp.bfloat16)
        )
        key_parts[kv_index] = key_parts[kv_index] + contract_first(shifted, query_head)
        value_parts[kv_index] = value_parts[kv_index] + contract_first(weights, grad_head)
    query_grad = jnp.concatenate(query_grads, 1)
    key_all = key_parts[0]
    value_all = value_parts[0]
    pieces = []
    for offset in range(steps_back + 1):
        lower = (steps_back - offset) * row_count
        pieces.append((key_all[lower : lower + row_count], value_all[lower : lower + row_count]))
    key_sum, value_sum = pieces[0]
    for offset in range(1, steps_back + 1):
        arrived = (
            from_behind(pieces[offset][0].astype(jnp.bfloat16), "ctx", -offset).astype(jnp.float32),
            from_behind(pieces[offset][1].astype(jnp.bfloat16), "ctx", -offset).astype(jnp.float32),
        )
        key_sum = key_sum + arrived[0]
        value_sum = value_sum + arrived[1]
    key_gradient = key_sum.astype(jnp.bfloat16)
    value_gradient = value_sum.astype(jnp.bfloat16)
    return (layer_output, query_grad, key_gradient, value_gradient, proj_grad)


def solution(mesh):
    in_specs = (
        P("ctx"),
        P("ctx", "hg"),
        P("ctx", "hg"),
        P("ctx", "hg"),
        P("ctx", "hg"),
        P("ctx", None),
    )
    out_specs = (P("ctx", "hg"), P("ctx", "hg"), P("ctx", "hg"), P("ctx", "hg"), P("ctx", "hg"))
    return jax.shard_map(body, mesh=mesh, in_specs=in_specs, out_specs=out_specs, check_vma=False)
```

profile of v0, /device:TPU:1, one launch (start us, length us, event | category | flops | bytes accessed | tf_op | source)
XLA Modules:
  0.0 323.6 jit_solution(5322077553955381528)
XLA Ops:
  7.2 0.7 all-gather.2.cloned.1.call-update
  7.9 4.0 %collective-permute-start.2 = (bf16[512,128]{1,0:T(8,128)(2,1)}, bf16[512,128]{1,0:T(8,128)(2,1)S(1)}, u32[]{:S(2)}, u32[]{:S(2)}) collective-permute-start(bf16[512,128]{1,0:T(8,128)(2,1)} %param.8), channel_id=1, source_target_pairs={{0,8},{4,12},{8,16},{12,20},{16,24},{20,28},{24,32},{28,36},{32,40... | collective-permute-start | bytes 393224 | tf_op jit(solution)/shard_map/ppermute | solution.py:14
  12.0 4.0 %collective-permute-start.3 = (bf16[512,128]{1,0:T(8,128)(2,1)}, bf16[512,128]{1,0:T(8,128)(2,1)S(1)}, u32[]{:S(2)}, u32[]{:S(2)}) collective-permute-start(bf16[512,128]{1,0:T(8,128)(2,1)} %param.8), channel_id=1, source_target_pairs={{0,4},{4,8},{8,12},{12,16},{16,20},{20,24},{24,28},{28,32},{32,36}... | collective-permute-start | bytes 393224 | tf_op jit(solution)/shard_map/ppermute | solution.py:14
  16.0 1.9 collective-permute-start.1
  18.0 2.9 collective-permute-start
  20.9 3.2 collective-permute-start.4
  24.1 4.1 %collective-permute-start.5 = (bf16[512,128]{1,0:T(8,128)(2,1)}, bf16[512,128]{1,0:T(8,128)(2,1)S(1)}, u32[]{:S(2)}, u32[]{:S(2)}) collective-permute-start(bf16[512,128]{1,0:T(8,128)(2,1)} %param.9), channel_id=1, source_target_pairs={{0,4},{4,8},{8,12},{12,16},{16,20},{20,24},{24,28},{28,32},{32,36}... | collective-permute-start | bytes 393224 | tf_op jit(solution)/shard_map/ppermute | solution.py:14
  28.3 0.7 pad_add_fusion
  29.1 0.9 constant_dynamic-update-slice_fusion
  30.0 0.5 collective-permute-done.5
  30.6 0.9 constant_dynamic-update-slice_fusion.3
  31.5 2.2 fusion.48
  33.8 1.2 fusion.49
  35.0 1.2 fusion.50
  36.1 1.2 fusion.51
  37.3 3.6 %select_reduce_fusion.3 = (f32[512]{0:T(512)S(1)}, f32[512]{0:T(512)S(1)}, f32[512]{0:T(512)S(1)}, f32[512]{0:T(512)S(1)}) fusion(f32[512,1536]{0,1:T(8,128)S(1)} %get-tuple-element.32, f32[512]{0:T(512)S(1)} %get-tuple-element.31, pred[1536]{0:T(1024)(128)(4,1)S(1)} %iota_compare_fusion.1, s32[1536]{0:T(1024)S(1)} %iota_add_fusion, ...), kind=kLoop, calls=%fused_computation.33 | loop fusion | flops 12580864 | bytes 12615168 | tf_op jit(solution)/shard_map/reduce_sum | solution.py:64
  40.9 4.0 %select_convert_fusion.3 = (bf16[512,1536]{0,1:T(8,128)(2,1)}, bf16[512,1536]{0,1:T(8,128)(2,1)S(1)}, bf16[512,1536]{0,1:T(8,128)(2,1)S(1)}, bf16[512,1536]{0,1:T(8,128)(2,1)S(1)}) fusion(f32[512,1536]{0,1:T(8,128)S(1)} %get-tuple-element.32, f32[512]{0:T(512)S(1)} %get-tuple-element.47, pred[1536]{0:T(1024)(128)(4,1)S(1)} %iota_compare_fusion.1, ...), kind=kLoop, calls=%fused_computation.32 | loop fusion | flops 12582912 | bytes 18898432 | tf_op jit(solution)/shard_map/convert_element_type | solution.py:66
  44.9 0.4 convolution_convert_fusion.6
  45.3 0.4 convolution_convert_fusion.7
  45.8 0.3 copy-done
  46.1 0.4 convolution_convert_fusion.8
  46.5 47.7 %all-gather.2.cloned.1.call-done = bf16[4096,512]{1,0:T(8,128)(2,1)} async-done(((bf16[64,512]{1,0:T(8,128)(2,1)}), bf16[4096,512]{1,0:T(8,128)(2,1)}) %all-gather.2.cloned.1.call-update) | async-done | bytes 4194320 | tf_op jit(solution)/shard_map/all_gather | solution.py:72
  94.2 6.0 %convolution_convert_fusion.1 = bf16[512,512]{0,1:T(8,128)(2,1)S(1)} fusion(bf16[512,4096]{1,0:T(8,128)(2,1)} %param.11, bf16[4096,512]{1,0:T(8,128)(2,1)} %all-gather.2.cloned.1.call-done), kind=kOutput, calls=%fused_computation.47 | convolution fusion | flops 2147745792 | bytes 8912896 | tf_op jit(solution)/shard_map/dot_general | solution.py:77
  100.2 0.5 multiply_reduce_fusion.3
  101.0 0.7 copy-done.18
  101.6 1.0 copy-done.6
  102.6 5.6 %convolution_bitcast_fusion = f32[4096,512]{0,1:T(8,128)} fusion(bf16[512,4096]{1,0:T(8,128)(2,1)S(1)} %copy-done.6, bf16[512,128]{0,1:T(8,128)(2,1)S(1)} %convolution_convert_fusion.6, bf16[512,128]{0,1:T(8,128)(2,1)S(1)} %convolution_convert_fusion.7, bf16[512,128]{0,1:T(8,128)(2,1)S(1)} %convolution_convert_fusion.8, bf16[512,128]{0,1:T(8,128)(2,1)S(1)} %get-tuple-element.39), kind=kOutput, calls=%fused_computation | convolution fusion | flops 2149580800 | bytes 13107200 | tf_op jit(solution)/shard_map/dot_general | solution.py:24
  108.2 9.0 %copy.27 = f32[4096,512]{1,0:T(8,128)} copy(f32[4096,512]{0,1:T(8,128)} %convolution_bitcast_fusion) | data formatting | bytes 16777216
  117.3 0.3 reduce-scatter.5.cloned.1.call-start
  117.6 6.6 %convolution_convert_fusion = bf16[512,4096]{1,0:T(8,128)(2,1)} fusion(bf16[4096,512]{1,0:T(8,128)(2,1)} %all-gather.2.cloned.1.call-done, bf16[512,128]{0,1:T(8,128)(2,1)S(1)} %convolution_convert_fusion.6, bf16[512,128]{0,1:T(8,128)(2,1)S(1)} %convolution_convert_fusion.7, bf16[512,128]{0,1:T(8,128)(2,1)S(1)} %convolution_convert_fusion.8, ...), kind=kOutput, calls=%fused_computation.1 | convolution fusion | flops 2151677952 | bytes 8912896 | tf_op jit(solution)/shard_map/dot_general | solution.py:18
  124.2 1.7 fusion.18
  126.0 1.2 copy-done.7
  127.2 0.4 convolution_convert_fusion.2
  127.6 0.6 fusion.19
  128.3 1.1 copy-done.9
  129.4 0.4 convolution_convert_fusion.3
  129.8 0.6 fusion.20
  130.5 0.4 convolution_convert_fusion.4
  130.9 0.4 copy-done.4
  131.3 0.6 fusion.21
  131.9 1.2 copy-done.12
  133.1 0.4 convolution_convert_fusion.5
  133.5 0.8 pad_maximum_fusion.1
  134.4 2.1 copy.21
  136.4 2.2 fusion.32
  138.6 2.1 convolution_add_fusion.5
  140.8 0.6 convolution_add_fusion.4
  141.4 0.6 fusion.52
  142.0 1.3 collective-permute-start.7
  143.3 2.2 collective-permute-start.6
  145.5 0.6 fusion.41
  146.1 0.6 convolution_add_fusion.2
  146.6 0.6 convolution_add_fusion.1
  147.2 0.6 fusion.53
  147.8 1.3 collective-permute-start.9
  149.1 1.9 collective-permute-start.8
  151.1 0.7 fusion.25
  151.8 4.2 %collective-permute-done.9 = bf16[512,128]{1,0:T(8,128)(2,1)S(1)} collective-permute-done((bf16[512,128]{1,0:T(8,128)(2,1)S(1)}, bf16[512,128]{1,0:T(8,128)(2,1)S(1)}, u32[]{:S(2)}, u32[]{:S(2)}) %collective-permute-start.9) | collective-permute-done | bytes 131104 | tf_op jit(solution)/shard_map/ppermute | solution.py:14
  155.9 1.3 collective-permute-done.8
  157.2 0.7 fusion.23
  157.9 103.7 %reduce-scatter.7.cloned.1.call-done = f32[64,512]{1,0:T(8,128)} async-done(((f32[4096,512]{1,0:T(8,128)}), f32[64,512]{1,0:T(8,128)}) %reduce-scatter.7.cloned.1.call-update) | async-done | bytes 131088
  261.6 1.0 copy.28
  262.7 0.7 copy.22
  263.4 53.7 %reduce-scatter.5.cloned.1.call-done = bf16[512,1024]{1,0:T(8,128)(2,1)} async-done(((bf16[512,4096]{1,0:T(8,128)(2,1)}), bf16[512,1024]{1,0:T(8,128)(2,1)}) %reduce-scatter.5.cloned.1.call-update) | async-done | bytes 1048592 | tf_op jit(solution)/shard_map/reduce_scatter | solution.py:73
  (64 shorter events, 0.6 us)
Async XLA Ops:
  7.2 87.0 %all-gather.2.cloned.1.call-start = ((), (), s32[]{:S(2)}) async-start(), calls=%async_computation.2 | async-start | bytes 4259840 | tf_op jit(solution)/shard_map/all_gather | solution.py:72
  7.9 253.8 %reduce-scatter.7.cloned.1.call-start = ((), (), s32[]{:S(2)}) async-start(), calls=%async_computation.4 | async-start | bytes 8519680
  7.9 21.1 %collective-permute-start.2 = (bf16[512,128]{1,0:T(8,128)(2,1)}, bf16[512,128]{1,0:T(8,128)(2,1)S(1)}, u32[]{:S(2)}, u32[]{:S(2)}) collective-permute-start(bf16[512,128]{1,0:T(8,128)(2,1)} %param.8), channel_id=1, source_target_pairs={{0,8},{4,12},{8,16},{12,20},{16,24},{20,28},{24,32},{28,36},{32,40... | collective-permute-start | bytes 393224 | tf_op jit(solution)/shard_map/ppermute | solution.py:14
  12.0 17.0 %collective-permute-start.3 = (bf16[512,128]{1,0:T(8,128)(2,1)}, bf16[512,128]{1,0:T(8,128)(2,1)S(1)}, u32[]{:S(2)}, u32[]{:S(2)}) collective-permute-start(bf16[512,128]{1,0:T(8,128)(2,1)} %param.8), channel_id=1, source_target_pairs={{0,4},{4,8},{8,12},{12,16},{16,20},{20,24},{24,28},{28,32},{32,36}... | collective-permute-start | bytes 393224 | tf_op jit(solution)/shard_map/ppermute | solution.py:14
  16.0 8.1 %collective-permute-start.1 = (s32[512]{0:T(512)}, s32[512]{0:T(512)S(1)}, u32[]{:S(2)}, u32[]{:S(2)}) collective-permute-start(s32[512]{0:T(512)} %param.6), channel_id=1, source_target_pairs={{0,4},{4,8},{8,12},{12,16},{16,20},{20,24},{24,28},{28,32},{32,36}... | collective-permute-start | bytes 6152 | tf_op jit(solution)/shard_map/ppermute | solution.py:14
  18.0 10.3 %collective-permute-start = (s32[512]{0:T(512)}, s32[512]{0:T(512)S(1)}, u32[]{:S(2)}, u32[]{:S(2)}) collective-permute-start(s32[512]{0:T(512)} %param.6), channel_id=1, source_target_pairs={{0,8},{4,12},{8,16},{12,20},{16,24},{20,28},{24,32},{28,36},{32,40... | collective-permute-start | bytes 6152 | tf_op jit(solution)/shard_map/ppermute | solution.py:14
  20.9 9.1 %collective-permute-start.4 = (bf16[512,128]{1,0:T(8,128)(2,1)}, bf16[512,128]{1,0:T(8,128)(2,1)S(1)}, u32[]{:S(2)}, u32[]{:S(2)}) collective-permute-start(bf16[512,128]{1,0:T(8,128)(2,1)} %param.9), channel_id=1, source_target_pairs={{0,8},{4,12},{8,16},{12,20},{16,24},{20,28},{24,32},{28,36},{32,40... | collective-permute-start | bytes 393224 | tf_op jit(solution)/shard_map/ppermute | solution.py:14
  24.1 6.4 %collective-permute-start.5 = (bf16[512,128]{1,0:T(8,128)(2,1)}, bf16[512,128]{1,0:T(8,128)(2,1)S(1)}, u32[]{:S(2)}, u32[]{:S(2)}) collective-permute-start(bf16[512,128]{1,0:T(8,128)(2,1)} %param.9), channel_id=1, source_target_pairs={{0,4},{4,8},{8,12},{12,16},{16,20},{20,24},{24,28},{28,32},{32,36}... | collective-permute-start | bytes 393224 | tf_op jit(solution)/shard_map/ppermute | solution.py:14
  30.0 6.2 %copy-start.19 = (bf16[1536,128]{1,0:T(8,128)(2,1)}, bf16[1536,128]{1,0:T(8,128)(2,1)S(1)}, u32[]{:S(2)}) copy-start(bf16[1536,128]{1,0:T(8,128)(2,1)S(1)} %constant_dynamic-update-slice_fusion) | copy-start | bytes 1179652
  31.5 14.3 %copy-start.21 = (bf16[1536,128]{1,0:T(8,128)(2,1)}, bf16[1536,128]{1,0:T(8,128)(2,1)S(1)}, u32[]{:S(2)}) copy-start(bf16[1536,128]{1,0:T(8,128)(2,1)S(1)} %constant_dynamic-update-slice_fusion.3) | copy-start | bytes 1179652
  31.5 2.3 copy-start.13
  31.5 2.3 copy-start.24
  44.9 1.2 copy-start
  94.2 6.0 %copy-start.3 = (bf16[512,1536]{0,1:T(8,128)(2,1)S(1)}, bf16[512,1536]{0,1:T(8,128)(2,1)}, u32[]{:S(2)}) copy-start(bf16[512,1536]{0,1:T(8,128)(2,1)} %get-tuple-element.27) | copy-start | bytes 4718596
  94.2 6.0 %copy-start.22 = (bf16[1536,128]{1,0:T(8,128)(2,1)S(1)}, bf16[1536,128]{1,0:T(8,128)(2,1)}, u32[]{:S(2)}) copy-start(bf16[1536,128]{1,0:T(8,128)(2,1)} %copy-done.21) | copy-start | bytes 1179652
  100.2 0.8 copy-start.15
  100.2 2.4 copy-start.6
  100.9 0.7 copy-start.18
  117.3 199.8 %reduce-scatter.5.cloned.1.call-start = ((), (), s32[]{:S(2)}) async-start(), calls=%async_computation.3 | async-start | bytes 5242880 | tf_op jit(solution)/shard_map/reduce_scatter | solution.py:73
  124.2 3.0 copy-start.20
  124.2 3.4 %copy-start.16 = (bf16[512,512]{0,1:T(8,128)(2,1)S(1)}, bf16[512,512]{0,1:T(8,128)(2,1)}, u32[]{:S(2)}) copy-start(bf16[512,512]{0,1:T(8,128)(2,1)} %copy-done.15) | copy-start | bytes 1572868
  124.2 3.4 %copy-start.23 = (bf16[1536,128]{1,0:T(8,128)(2,1)S(1)}, bf16[1536,128]{1,0:T(8,128)(2,1)}, u32[]{:S(2)}) copy-start(bf16[1536,128]{1,0:T(8,128)(2,1)} %copy-done.21) | copy-start | bytes 1179652
  126.0 1.2 copy-start.7
  127.6 2.2 copy-start.1
  128.2 1.1 copy-start.9
  129.8 1.5 copy-start.4
  130.5 3.0 copy-start.11
  131.9 1.2 copy-start.12
  136.4 4.3 %copy-start.10 = (bf16[512,1536]{0,1:T(8,128)(2,1)S(1)}, bf16[512,1536]{0,1:T(8,128)(2,1)}, u32[]{:S(2)}) copy-start(bf16[512,1536]{0,1:T(8,128)(2,1)} %copy-done.9) | copy-start | bytes 4718596
  136.4 4.3 %copy-start.14 = (bf16[512,512]{1,0:T(8,128)(2,1)S(1)}, bf16[512,512]{1,0:T(8,128)(2,1)}, u32[]{:S(2)}) copy-start(bf16[512,512]{1,0:T(8,128)(2,1)} %param.7) | copy-start | bytes 1572868
  138.6 2.8 copy-start.8
  140.8 4.7 %copy-start.5 = (bf16[512,1536]{0,1:T(8,128)(2,1)S(1)}, bf16[512,1536]{0,1:T(8,128)(2,1)}, u32[]{:S(2)}) copy-start(bf16[512,1536]{0,1:T(8,128)(2,1)} %get-tuple-element.27) | copy-start | bytes 4718596
  140.8 4.7 %copy-start.17 = (bf16[512,512]{0,1:T(8,128)(2,1)S(1)}, bf16[512,512]{0,1:T(8,128)(2,1)}, u32[]{:S(2)}) copy-start(bf16[512,512]{0,1:T(8,128)(2,1)} %copy-done.15) | copy-start | bytes 1572868
  141.4 4.7 %copy-start.2 = (bf16[512,1536]{0,1:T(8,128)(2,1)S(1)}, bf16[512,1536]{0,1:T(8,128)(2,1)}, u32[]{:S(2)}) copy-start(bf16[512,1536]{0,1:T(8,128)(2,1)} %copy-done) | copy-start | bytes 4718596
  142.0 9.0 %collective-permute-start.7 = (bf16[512,128]{1,0:T(8,128)(2,1)S(1)}, bf16[512,128]{1,0:T(8,128)(2,1)S(1)}, u32[]{:S(2)}, u32[]{:S(2)}) collective-permute-start(bf16[512,128]{1,0:T(8,128)(2,1)S(1)} %get-tuple-element.26), channel_id=1, source_target_pairs={{8,0},{12,4},{16,8},{20,12},{24,16},{28,20},{32,24},{36,28},{40,32... | collective-permute-start | bytes 393224 | tf_op jit(solution)/shard_map/ppermute | solution.py:14
  143.3 7.8 %collective-permute-start.6 = (bf16[512,128]{1,0:T(8,128)(2,1)S(1)}, bf16[512,128]{1,0:T(8,128)(2,1)S(1)}, u32[]{:S(2)}, u32[]{:S(2)}) collective-permute-start(bf16[512,128]{1,0:T(8,128)(2,1)S(1)} %get-tuple-element.25), channel_id=1, source_target_pairs={{4,0},{8,4},{12,8},{16,12},{20,16},{24,20},{28,24},{32,28},{36,32}... | collective-permute-start | bytes 393224 | tf_op jit(solution)/shard_map/ppermute | solution.py:14
  147.8 8.1 %collective-permute-start.9 = (bf16[512,128]{1,0:T(8,128)(2,1)S(1)}, bf16[512,128]{1,0:T(8,128)(2,1)S(1)}, u32[]{:S(2)}, u32[]{:S(2)}) collective-permute-start(bf16[512,128]{1,0:T(8,128)(2,1)S(1)} %get-tuple-element.24), channel_id=1, source_target_pairs={{8,0},{12,4},{16,8},{20,12},{24,16},{28,20},{32,24},{36,28},{40,32... | collective-permute-start | bytes 393224 | tf_op jit(solution)/shard_map/ppermute | solution.py:14
  149.1 8.1 %collective-permute-start.8 = (bf16[512,128]{1,0:T(8,128)(2,1)S(1)}, bf16[512,128]{1,0:T(8,128)(2,1)S(1)}, u32[]{:S(2)}, u32[]{:S(2)}) collective-permute-start(bf16[512,128]{1,0:T(8,128)(2,1)S(1)} %get-tuple-element.23), channel_id=1, source_target_pairs={{4,0},{8,4},{12,8},{16,12},{20,16},{24,20},{28,24},{32,28},{36,32}... | collective-permute-start | bytes 393224 | tf_op jit(solution)/shard_map/ppermute | solution.py:14
Sparse Core Ops, SparseCore 0:
  10.7 83.4 all-gather.1
  117.4 144.2 reduce-scatter.6
  264.8 52.2 reduce-scatter.4
where the time goes:
time: 324 us
  waiting for transfers between devices  212 us (65%)
  matrix products  38.7 us (12%)
  starting transfers between devices  27.3 us (8%)
  local copies, waits for them, and re-layouts  20.9 us (6%)
  between operations  14.4 us (4%)
  other arithmetic  10.5 us (3%)
    unnamed x4, waiting for transfers between devices  104 us
    reduce_scatter x1, waiting for transfers between devices, body(): lax.psum_scatter(partial_value.astype(jnp.bfloat16), 'hg', scatter_dimens...  53.7 us
    all_gather x1, waiting for transfers between devices, body(): lax.all_gather(out_proj, 'ctx', axis=0, tiled=True)  47.7 us
    ppermute x10, starting transfers between devices, from_behind(): return lax.ppermute(value, axis, pairs)  26.9 us
    unnamed x58, local copies, waits for them, and re-layouts  19 us
    dot_general x9, matrix products, contract_last(): lax.dot_general(left_side, right_side, (((1,), (1,)), ((), ())), preferre...  16 us
    dot_general x9, matrix products, contract_first(): lax.dot_general(left_side, right_side, (((0,), (0,)), ((), ())), preferre...  13.3 us
  transfers between devices with their start and end apart: 13, of which 6 were waited for; matrix products, arithmetic and copies ran while one was open for 13% of the time, Pallas kernels for 0%

commit v1 on v0

--- a/solution.py
+++ b/solution.py
@@ -6,6 +6,11 @@
 HEAD_SIZE = 128
 TOK_DEV = 512
 DOC_MOST = 1024
+
+
+def exchange_gather(array, name, along):
+    stack = jnp.stack([array] * lax.axis_size(name))
+    return jnp.concatenate(lax.all_to_all(stack, name, 0, 0), axis=along)
 
 
 def from_behind(value, axis, by):
@@ -69,7 +74,7 @@
             jnp.dot(weights, value_head, preferred_element_type=jnp.float32).astype(jnp.bfloat16)
         )
     attended = jnp.concatenate(outputs, 1)
-    partial_value = contract_last(attended, lax.all_gather(out_proj, "ctx", axis=0, tiled=True))
+    partial_value = contract_last(attended, exchange_gather(out_proj, "ctx", 0))
     layer_output = lax.psum_scatter(
         partial_value.astype(jnp.bfloat16), "hg", scatter_dimension=1, tiled=True
     )

time: 324 us -> 339 us (1.046)
  blocking collectives: 0 us -> 109 us
  waiting for transfers between devices: 212 us -> 114 us
    all_to_all x0 -> x1, blocking collectives: none -> 109 us  [exchange_gather(): return jnp.concatenate(lax.all_to_all(stack, name, 0, 0), axis=along)]
    unnamed x4, waiting for transfers between devices: 104 us -> 6.17 us
    unnamed x58 -> x68, local copies, waits for them, and re-layouts: 19 us -> 21.4 us
  transfers between devices with their start and end apart: 13 -> 13, of which waited for: 6 -> 7; matrix products, arithmetic and copies ran while one was open for 13% -> 12% of each run, Pallas kernels for 0% -> 0%
where the time goes in v1:
time: 339 us; the launch traced here: 338 us
  waiting for transfers between devices  114 us (34%)
  blocking collectives  109 us (32%)
  matrix products  36.2 us (11%)
  starting transfers between devices  29.5 us (9%)
  local copies, waits for them, and re-layouts  23.9 us (7%)
  between operations  14.4 us (4%)
  other arithmetic  10.5 us (3%)
    all_to_all x1, blocking collectives, exchange_gather(): return jnp.concatenate(lax.all_to_all(stack, name, 0, 0), axis=along)  109 us
    reduce_scatter x1, waiting for transfers between devices, body(): lax.psum_scatter(partial_value.astype(jnp.bfloat16), 'hg', scatter_dimens...  53.3 us
    all_gather x1, waiting for transfers between devices, body(): lax.all_gather(out_proj, 'ctx', axis=0, tiled=True)  45.3 us
    ppermute x10, starting transfers between devices, from_behind(): return lax.ppermute(value, axis, pairs)  29.4 us
    unnamed x68, local copies, waits for them, and re-layouts  21.4 us
    dot_general x9, matrix products, contract_last(): lax.dot_general(left_side, right_side, (((1,), (1,)), ((), ())), preferre...  13.5 us
    dot_general x9, matrix products, contract_first(): lax.dot_general(left_side, right_side, (((0,), (0,)), ((), ())), preferre...  12.6 us
    ppermute x10, waiting for transfers between devices, from_behind(): return lax.ppermute(value, axis, pairs)  9.06 us
  transfers between devices with their start and end apart: 13, of which 7 were waited for; matrix products, arithmetic and copies ran while one was open for 12% of the time, Pallas kernels for 0%

profile of v1, /device:TPU:1, one launch (start us, length us, event | category | flops | bytes accessed | tf_op | source)
XLA Modules:
  0.0 337.7 jit_solution(4651847398898579982)
XLA Ops:
  7.2 0.7 all-gather.2.cloned.1.call-update
  7.9 4.0 %collective-permute-start = (s32[512]{0:T(512)}, s32[512]{0:T(512)S(1)}, u32[]{:S(2)}, u32[]{:S(2)}) collective-permute-start(s32[512]{0:T(512)} %param.6), channel_id=1, source_target_pairs={{0,8},{4,12},{8,16},{12,20},{16,24},{20,28},{24,32},{28,36},{32,40... | collective-permute-start | bytes 6152 | tf_op jit(solution)/shard_map/ppermute | solution.py:19
  12.0 4.1 %collective-permute-start.1 = (s32[512]{0:T(512)}, s32[512]{0:T(512)S(1)}, u32[]{:S(2)}, u32[]{:S(2)}) collective-permute-start(s32[512]{0:T(512)} %param.6), channel_id=1, source_target_pairs={{0,4},{4,8},{8,12},{12,16},{16,20},{20,24},{24,28},{28,32},{32,36}... | collective-permute-start | bytes 6152 | tf_op jit(solution)/shard_map/ppermute | solution.py:19
  16.0 2.9 collective-permute-start.2
  19.0 2.2 collective-permute-start.3
  21.2 3.2 collective-permute-start.4
  24.4 3.6 %collective-permute-start.5 = (bf16[512,128]{1,0:T(8,128)(2,1)}, bf16[512,128]{1,0:T(8,128)(2,1)S(1)}, u32[]{:S(2)}, u32[]{:S(2)}) collective-permute-start(bf16[512,128]{1,0:T(8,128)(2,1)} %param.9), channel_id=1, source_target_pairs={{0,4},{4,8},{8,12},{12,16},{16,20},{20,24},{24,28},{28,32},{32,36}... | collective-permute-start | bytes 393224 | tf_op jit(solution)/shard_map/ppermute | solution.py:19
  28.0 0.7 pad_add_fusion
  28.7 1.6 collective-permute-done.5
  30.4 0.9 constant_dynamic-update-slice_fusion.3
  31.4 1.0 constant_dynamic-update-slice_fusion
  32.4 2.2 fusion.51
  34.7 1.2 fusion.50
  35.9 1.2 fusion.49
  37.1 1.2 fusion.48
  38.2 3.6 %select_reduce_fusion.3 = (f32[512]{0:T(512)S(1)}, f32[512]{0:T(512)S(1)}, f32[512]{0:T(512)S(1)}, f32[512]{0:T(512)S(1)}) fusion(f32[512,1536]{0,1:T(8,128)S(1)} %get-tuple-element.32, f32[512]{0:T(512)S(1)} %get-tuple-element.31, pred[1536]{0:T(1024)(128)(4,1)S(1)} %iota_compare_fusion.1, s32[1536]{0:T(1024)S(1)} %iota_add_fusion, ...), kind=kLoop, calls=%fused_computation.33 | loop fusion | flops 12580864 | bytes 12615168 | tf_op jit(solution)/shard_map/reduce_sum | solution.py:69
  41.8 4.0 %select_convert_fusion.3 = (bf16[512,1536]{0,1:T(8,128)(2,1)}, bf16[512,1536]{0,1:T(8,128)(2,1)S(1)}, bf16[512,1536]{0,1:T(8,128)(2,1)S(1)}, bf16[512,1536]{0,1:T(8,128)(2,1)S(1)}) fusion(f32[512,1536]{0,1:T(8,128)S(1)} %get-tuple-element.32, f32[512]{0:T(512)S(1)} %get-tuple-element.47, pred[1536]{0:T(1024)(128)(4,1)S(1)} %iota_compare_fusion.1, ...), kind=kLoop, calls=%fused_computation.32 | loop fusion | flops 12582912 | bytes 18898432 | tf_op jit(solution)/shard_map/convert_element_type | solution.py:71
  45.8 1.1 copy-done
  47.4 0.4 convolution_convert_fusion.7
  47.8 1.1 convolution_convert_fusion.6
  48.9 45.3 %all-gather.2.cloned.1.call-done = bf16[4096,512]{1,0:T(8,128)(2,1)} async-done(((bf16[64,512]{1,0:T(8,128)(2,1)}), bf16[4096,512]{1,0:T(8,128)(2,1)}) %all-gather.2.cloned.1.call-update) | async-done | bytes 4194320 | tf_op jit(solution)/shard_map/all_gather | solution.py:84
  94.2 6.0 %convolution_convert_fusion.1 = bf16[512,512]{0,1:T(8,128)(2,1)S(1)} fusion(bf16[512,4096]{1,0:T(8,128)(2,1)} %param.11, bf16[4096,512]{1,0:T(8,128)(2,1)} %all-gather.2.cloned.1.call-done), kind=kOutput, calls=%fused_computation.47 | convolution fusion | flops 2147745792 | bytes 8912896 | tf_op jit(solution)/shard_map/dot_general | solution.py:82
  100.2 0.5 multiply_reduce_fusion.3
  101.0 0.7 copy-done.22
  101.6 1.0 copy-done.5
  102.6 5.6 %convolution_bitcast_fusion = f32[4096,512]{0,1:T(8,128)} fusion(bf16[512,4096]{1,0:T(8,128)(2,1)S(1)} %copy-done.5, bf16[512,128]{0,1:T(8,128)(2,1)S(1)} %copy-done.20, bf16[512,128]{0,1:T(8,128)(2,1)S(1)} %convolution_convert_fusion.7, bf16[512,128]{0,1:T(8,128)(2,1)S(1)} %convolution_convert_fusion.8, bf16[512,128]{0,1:T(8,128)(2,1)S(1)} %get-tuple-element.39), kind=kOutput, calls=%fused_computation | convolution fusion | flops 2149580800 | bytes 13107200 | tf_op jit(solution)/shard_map/dot_general | solution.py:29
  108.2 9.0 %copy.27 = f32[4096,512]{1,0:T(8,128)} copy(f32[4096,512]{0,1:T(8,128)} %convolution_bitcast_fusion) | data formatting | bytes 16777216
  117.3 0.8 copy-done.19
  118.1 0.5 stack.2
  118.6 109.5 %all_to_all.5 = bf16[64,64,512]{2,1,0:T(8,128)(2,1)S(1)} all-to-all(bf16[64,64,512]{2,1,0:T(8,128)(2,1)S(1)} %stack.2), channel_id=1, replica_groups=mesh['ctx'=64,'hg'=4] {'ctx'}, dimensions={0} | all-to-all | bytes 8388608 | tf_op jit(solution)/shard_map/all_to_all | solution.py:13
  228.1 4.4 %convolution_convert_fusion = bf16[512,4096]{1,0:T(8,128)(2,1)} fusion(bf16[4096,512]{1,0:T(8,128)(2,1)S(1)} %bitcast.56, bf16[512,128]{0,1:T(8,128)(2,1)S(1)} %copy-done.21, bf16[512,128]{0,1:T(8,128)(2,1)S(1)} %convolution_convert_fusion.7, bf16[512,128]{0,1:T(8,128)(2,1)S(1)} %convolution_convert_fusion.8, bf16[512,128]{0,1:T(8,128)(2,1)S(1)} %copy-done.23), kind=kOutput, calls=%fused_computation.1 | convolution fusion | flops 2151677952 | bytes 8912896 | tf_op jit(solution)/shard_map/dot_general | solution.py:23
  232.6 0.9 copy-done.26
  233.5 1.5 fusion.19
  235.0 1.2 copy-done.8
  236.2 0.4 convolution_convert_fusion.3
  236.7 0.6 fusion.20
  238.1 0.6 fusion.21
  238.7 0.4 convolution_convert_fusion.5
  239.1 0.7 copy-done.12
  239.9 0.6 fusion.18
  240.5 1.1 copy-done.6
  242.1 0.8 pad_maximum_fusion.1
  242.9 2.0 copy.21
  244.9 2.1 fusion.41
  247.1 1.5 convolution_add_fusion.2
  248.6 0.6 convolution_add_fusion.1
  249.2 0.6 fusion.53
  249.8 4.9 %collective-permute-start.8 = (bf16[512,128]{1,0:T(8,128)(2,1)S(1)}, bf16[512,128]{1,0:T(8,128)(2,1)S(1)}, u32[]{:S(2)}, u32[]{:S(2)}) collective-permute-start(bf16[512,128]{1,0:T(8,128)(2,1)S(1)} %get-tuple-element.23), channel_id=1, source_target_pairs={{4,0},{8,4},{12,8},{16,12},{20,16},{24,20},{28,24},{32,28},{36,32}... | collective-permute-start | bytes 393224 | tf_op jit(solution)/shard_map/ppermute | solution.py:19
  254.7 1.3 collective-permute-start.9
  256.0 0.6 fusion.32
  256.6 0.6 convolution_add_fusion.5
  257.2 0.6 convolution_add_fusion.4
  258.0 0.6 fusion.52
  258.6 1.9 collective-permute-start.6
  260.5 1.3 collective-permute-start.7
  261.8 1.6 collective-permute-done.9
  263.5 0.7 fusion.23
  264.2 2.1 collective-permute-done.6
  266.3 3.7 %collective-permute-done.7 = bf16[512,128]{1,0:T(8,128)(2,1)S(1)} collective-permute-done((bf16[512,128]{1,0:T(8,128)(2,1)S(1)}, bf16[512,128]{1,0:T(8,128)(2,1)S(1)}, u32[]{:S(2)}, u32[]{:S(2)}) %collective-permute-start.7) | collective-permute-done | bytes 131104 | tf_op jit(solution)/shard_map/ppermute | solution.py:19
  270.0 0.7 fusion.25
  270.7 5.5 %reduce-scatter.7.cloned.1.call-done = f32[64,512]{1,0:T(8,128)} async-done(((f32[4096,512]{1,0:T(8,128)}), f32[64,512]{1,0:T(8,128)}) %reduce-scatter.7.cloned.1.call-update) | async-done | bytes 131088
  276.1 1.0 copy.28
  277.2 0.7 copy.22
  277.9 53.3 %reduce-scatter.5.cloned.1.call-done = bf16[512,1024]{1,0:T(8,128)(2,1)} async-done(((bf16[512,4096]{1,0:T(8,128)(2,1)}), bf16[512,1024]{1,0:T(8,128)(2,1)}) %reduce-scatter.5.cloned.1.call-update) | async-done | bytes 1048592 | tf_op jit(solution)/shard_map/reduce_scatter | solution.py:78
  (76 shorter events, 2.5 us)
Async XLA Ops:
  7.2 87.0 %all-gather.2.cloned.1.call-start = ((), (), s32[]{:S(2)}) async-start(), calls=%async_computation.4 | async-start | bytes 4259840 | tf_op jit(solution)/shard_map/all_gather | solution.py:84
  7.9 268.2 %reduce-scatter.7.cloned.1.call-start = ((), (), s32[]{:S(2)}) async-start(), calls=%async_computation.5 | async-start | bytes 8519680
  7.9 16.5 %collective-permute-start = (s32[512]{0:T(512)}, s32[512]{0:T(512)S(1)}, u32[]{:S(2)}, u32[]{:S(2)}) collective-permute-start(s32[512]{0:T(512)} %param.6), channel_id=1, source_target_pairs={{0,8},{4,12},{8,16},{12,20},{16,24},{20,28},{24,32},{28,36},{32,40... | collective-permute-start | bytes 6152 | tf_op jit(solution)/shard_map/ppermute | solution.py:19
  12.0 16.1 %collective-permute-start.1 = (s32[512]{0:T(512)}, s32[512]{0:T(512)S(1)}, u32[]{:S(2)}, u32[]{:S(2)}) collective-permute-start(s32[512]{0:T(512)} %param.6), channel_id=1, source_target_pairs={{0,4},{4,8},{8,12},{12,16},{16,20},{20,24},{24,28},{28,32},{32,36}... | collective-permute-start | bytes 6152 | tf_op jit(solution)/shard_map/ppermute | solution.py:19
  16.0 15.3 %collective-permute-start.2 = (bf16[512,128]{1,0:T(8,128)(2,1)}, bf16[512,128]{1,0:T(8,128)(2,1)S(1)}, u32[]{:S(2)}, u32[]{:S(2)}) collective-permute-start(bf16[512,128]{1,0:T(8,128)(2,1)} %param.8), channel_id=1, source_target_pairs={{0,8},{4,12},{8,16},{12,20},{16,24},{20,28},{24,32},{28,36},{32,40... | collective-permute-start | bytes 393224 | tf_op jit(solution)/shard_map/ppermute | solution.py:19
  19.0 12.4 %collective-permute-start.3 = (bf16[512,128]{1,0:T(8,128)(2,1)}, bf16[512,128]{1,0:T(8,128)(2,1)S(1)}, u32[]{:S(2)}, u32[]{:S(2)}) collective-permute-start(bf16[512,128]{1,0:T(8,128)(2,1)} %param.8), channel_id=1, source_target_pairs={{0,4},{4,8},{8,12},{12,16},{16,20},{20,24},{24,28},{28,32},{32,36}... | collective-permute-start | bytes 393224 | tf_op jit(solution)/shard_map/ppermute | solution.py:19
  21.2 7.6 %collective-permute-start.4 = (bf16[512,128]{1,0:T(8,128)(2,1)}, bf16[512,128]{1,0:T(8,128)(2,1)S(1)}, u32[]{:S(2)}, u32[]{:S(2)}) collective-permute-start(bf16[512,128]{1,0:T(8,128)(2,1)} %param.9), channel_id=1, source_target_pairs={{0,8},{4,12},{8,16},{12,20},{16,24},{20,28},{24,32},{28,36},{32,40... | collective-permute-start | bytes 393224 | tf_op jit(solution)/shard_map/ppermute | solution.py:19
  24.4 5.9 %collective-permute-start.5 = (bf16[512,128]{1,0:T(8,128)(2,1)}, bf16[512,128]{1,0:T(8,128)(2,1)S(1)}, u32[]{:S(2)}, u32[]{:S(2)}) collective-permute-start(bf16[512,128]{1,0:T(8,128)(2,1)} %param.9), channel_id=1, source_target_pairs={{0,4},{4,8},{8,12},{12,16},{16,20},{20,24},{24,28},{28,32},{32,36}... | collective-permute-start | bytes 393224 | tf_op jit(solution)/shard_map/ppermute | solution.py:19
  31.3 16.5 %copy-start.24 = (bf16[1536,128]{1,0:T(8,128)(2,1)}, bf16[1536,128]{1,0:T(8,128)(2,1)S(1)}, u32[]{:S(2)}) copy-start(bf16[1536,128]{1,0:T(8,128)(2,1)S(1)} %constant_dynamic-update-slice_fusion.3) | copy-start | bytes 1179652
  32.4 4.7 %copy-start.27 = (bf16[1536,128]{1,0:T(8,128)(2,1)}, bf16[1536,128]{1,0:T(8,128)(2,1)S(1)}, u32[]{:S(2)}) copy-start(bf16[1536,128]{1,0:T(8,128)(2,1)S(1)} %constant_dynamic-update-slice_fusion) | copy-start | bytes 1179652
  32.4 2.3 copy-start.14
  32.4 2.3 copy-start.29
  45.8 1.1 copy-start
  94.2 6.0 %copy-start.3 = (bf16[512,1536]{0,1:T(8,128)(2,1)S(1)}, bf16[512,1536]{0,1:T(8,128)(2,1)}, u32[]{:S(2)}) copy-start(bf16[512,1536]{0,1:T(8,128)(2,1)} %get-tuple-element.27) | copy-start | bytes 4718596
  94.2 6.0 %copy-start.20 = (bf16[512,128]{0,1:T(8,128)(2,1)S(1)}, bf16[512,128]{0,1:T(8,128)(2,1)}, u32[]{:S(2)}) copy-start(bf16[512,128]{0,1:T(8,128)(2,1)} %convolution_convert_fusion.6) | copy-start | bytes 393220
  94.2 6.0 %copy-start.25 = (bf16[1536,128]{1,0:T(8,128)(2,1)S(1)}, bf16[1536,128]{1,0:T(8,128)(2,1)}, u32[]{:S(2)}) copy-start(bf16[1536,128]{1,0:T(8,128)(2,1)} %copy-done.24) | copy-start | bytes 1179652
  100.2 0.8 copy-start.16
  100.2 2.4 copy-start.5
  101.0 0.7 copy-start.22
  117.3 0.8 copy-start.19
  117.3 213.9 %reduce-scatter.5.cloned.1.call-start = ((), (), s32[]{:S(2)}) async-start(), calls=%async_computation.3 | async-start | bytes 5242880 | tf_op jit(solution)/shard_map/reduce_scatter | solution.py:78
  118.6 109.5 %copy-start.21 = (bf16[512,128]{0,1:T(8,128)(2,1)S(1)}, bf16[512,128]{0,1:T(8,128)(2,1)}, u32[]{:S(2)}) copy-start(bf16[512,128]{0,1:T(8,128)(2,1)} %convolution_convert_fusion.6) | copy-start | bytes 393220
  118.6 109.5 %copy-start.23 = (bf16[512,128]{0,1:T(8,128)(2,1)S(1)}, bf16[512,128]{0,1:T(8,128)(2,1)}, u32[]{:S(2)}) copy-start(bf16[512,128]{0,1:T(8,128)(2,1)} %copy-done.22) | copy-start | bytes 393220
  232.5 1.0 copy-start.26
  232.5 3.7 %copy-start.28 = (bf16[1536,128]{1,0:T(8,128)(2,1)S(1)}, bf16[1536,128]{1,0:T(8,128)(2,1)}, u32[]{:S(2)}) copy-start(bf16[1536,128]{1,0:T(8,128)(2,1)} %copy-done.27) | copy-start | bytes 1179652
  232.5 4.1 %copy-start.1 = (bf16[512,1536]{0,1:T(8,128)(2,1)S(1)}, bf16[512,1536]{0,1:T(8,128)(2,1)}, u32[]{:S(2)}) copy-start(bf16[512,1536]{0,1:T(8,128)(2,1)} %copy-done) | copy-start | bytes 4718596
  232.5 4.1 %copy-start.17 = (bf16[512,512]{0,1:T(8,128)(2,1)S(1)}, bf16[512,512]{0,1:T(8,128)(2,1)}, u32[]{:S(2)}) copy-start(bf16[512,512]{0,1:T(8,128)(2,1)} %copy-done.16) | copy-start | bytes 1572868
  235.0 1.2 copy-start.8
  236.6 1.4 copy-start.4
  237.3 1.8 copy-start.10
  238.7 1.2 copy-start.12
  240.5 1.2 copy-start.6
  244.9 2.1 copy-start.2
  244.9 3.6 %copy-start.18 = (bf16[512,512]{0,1:T(8,128)(2,1)S(1)}, bf16[512,512]{0,1:T(8,128)(2,1)}, u32[]{:S(2)}) copy-start(bf16[512,512]{0,1:T(8,128)(2,1)} %copy-done.16) | copy-start | bytes 1572868
  248.6 7.4 %copy-start.13 = (bf16[512,1536]{0,1:T(8,128)(2,1)S(1)}, bf16[512,1536]{0,1:T(8,128)(2,1)}, u32[]{:S(2)}) copy-start(bf16[512,1536]{0,1:T(8,128)(2,1)} %copy-done.12) | copy-start | bytes 4718596
  248.6 7.4 %copy-start.15 = (bf16[512,512]{1,0:T(8,128)(2,1)S(1)}, bf16[512,512]{1,0:T(8,128)(2,1)}, u32[]{:S(2)}) copy-start(bf16[512,512]{1,0:T(8,128)(2,1)} %param.7) | copy-start | bytes 1572868
  249.2 7.4 %copy-start.11 = (bf16[512,1536]{0,1:T(8,128)(2,1)S(1)}, bf16[512,1536]{0,1:T(8,128)(2,1)}, u32[]{:S(2)}) copy-start(bf16[512,1536]{0,1:T(8,128)(2,1)} %copy-done.10) | copy-start | bytes 4718596
  249.8 7.4 %copy-start.9 = (bf16[512,1536]{0,1:T(8,128)(2,1)S(1)}, bf16[512,1536]{0,1:T(8,128)(2,1)}, u32[]{:S(2)}) copy-start(bf16[512,1536]{0,1:T(8,128)(2,1)} %copy-done.8) | copy-start | bytes 4718596
  249.8 12.0 %collective-permute-start.8 = (bf16[512,128]{1,0:T(8,128)(2,1)S(1)}, bf16[512,128]{1,0:T(8,128)(2,1)S(1)}, u32[]{:S(2)}, u32[]{:S(2)}) collective-permute-start(bf16[512,128]{1,0:T(8,128)(2,1)S(1)} %get-tuple-element.23), channel_id=1, source_target_pairs={{4,0},{8,4},{12,8},{16,12},{20,16},{24,20},{28,24},{32,28},{36,32}... | collective-permute-start | bytes 393224 | tf_op jit(solution)/shard_map/ppermute | solution.py:19
  254.7 8.8 %collective-permute-start.9 = (bf16[512,128]{1,0:T(8,128)(2,1)S(1)}, bf16[512,128]{1,0:T(8,128)(2,1)S(1)}, u32[]{:S(2)}, u32[]{:S(2)}) collective-permute-start(bf16[512,128]{1,0:T(8,128)(2,1)S(1)} %get-tuple-element.24), channel_id=1, source_target_pairs={{8,0},{12,4},{16,8},{20,12},{24,16},{28,20},{32,24},{36,28},{40,32... | collective-permute-start | bytes 393224 | tf_op jit(solution)/shard_map/ppermute | solution.py:19
  256.6 1.4 copy-start.7
  258.6 7.7 %collective-permute-start.6 = (bf16[512,128]{1,0:T(8,128)(2,1)S(1)}, bf16[512,128]{1,0:T(8,128)(2,1)S(1)}, u32[]{:S(2)}, u32[]{:S(2)}) collective-permute-start(bf16[512,128]{1,0:T(8,128)(2,1)S(1)} %get-tuple-element.25), channel_id=1, source_target_pairs={{4,0},{8,4},{12,8},{16,12},{20,16},{24,20},{28,24},{32,28},{36,32}... | collective-permute-start | bytes 393224 | tf_op jit(solution)/shard_map/ppermute | solution.py:19
  260.5 9.4 %collective-permute-start.7 = (bf16[512,128]{1,0:T(8,128)(2,1)S(1)}, bf16[512,128]{1,0:T(8,128)(2,1)S(1)}, u32[]{:S(2)}, u32[]{:S(2)}) collective-permute-start(bf16[512,128]{1,0:T(8,128)(2,1)S(1)} %get-tuple-element.26), channel_id=1, source_target_pairs={{8,0},{12,4},{16,8},{20,12},{24,16},{28,20},{32,24},{36,28},{40,32... | collective-permute-start | bytes 393224 | tf_op jit(solution)/shard_map/ppermute | solution.py:19
Sparse Core Ops, SparseCore 0:
  10.7 83.3 all-gather.1
  117.4 158.6 reduce-scatter.6
  279.3 51.8 reduce-scatter.4
